TPU v7x, 32 devices: a whole 2x2x4 slice. The times are simulated.
32 devices in a mesh: grp: 4 (over z), shard: 8 (over y, x, core).
Axes of the slice: x: 2, y: 2, z: 4, core: 2. Of those that a mesh axis runs over, the one named last changes fastest.
Arguments:
- table: float32 [1024, 8, 128], P('shard')
- table_first: float32 [1024, 8, 128], P('shard'), may hold values from -3 to 3
- table_second: float32 [1024, 8, 128], P('shard')
- slot_table: int32 [1024], P('shard'), may hold values from 0 to 25
- touched: int32 [4, 256], P('grp', 'shard'), may hold values from 0 to 1023, as said below
- emb_grads: bfloat16 [4, 256, 8, 128], P('grp', 'shard'), may hold values from -6 to 6
- block_slot: int32 [1024], replicated, may hold values from 0 to 1023, as said below
- dense_x: bfloat16 [13, 131072], P(None, ('grp', 'shard')), may hold values from -6 to 6
- dense_cot: bfloat16 [131072, 128], P(('grp', 'shard')), may hold values from -0.15625 to 0.15625
- w_one: float32 [13, 512], replicated, may hold values from -1.75 to 1.75
- w_two: float32 [512, 256], replicated, may hold values from -0.25 to 0.25
- w_three: float32 [256, 128], replicated, may hold values from -0.375 to 0.375
- first_one: float32 [13, 512], replicated, may hold values from -3 to 3
- first_two: float32 [512, 256], replicated, may hold values from -3 to 3
- first_three: float32 [256, 128], replicated, may hold values from -3 to 3
- second_one: float32 [13, 512], replicated, may hold values from 0.001 to 0.3
- second_two: float32 [512, 256], replicated, may hold values from 0.001 to 0.3
- second_three: float32 [256, 128], replicated, may hold values from 0.001 to 0.3
Outputs:
- new_table: float32 [1024, 8, 128], P('shard')
- new_table_first: float32 [1024, 8, 128], P('shard')
- new_table_second: float32 [1024, 8, 128], P('shard')
- new_w_one: float32 [13, 512], replicated
- new_w_two: float32 [512, 256], replicated
- new_w_three: float32 [256, 128], replicated
- new_first_one: float32 [13, 512], replicated
- new_first_two: float32 [512, 256], replicated
- new_first_three: float32 [256, 128], replicated
- new_second_one: float32 [13, 512], replicated
- new_second_two: float32 [512, 256], replicated
- new_second_three: float32 [256, 128], replicated
Inputs may be any that keep to these rules, and one draw needn't show every extreme that they name: `touched`: each device's 32 ids are distinct; at most 8 of them have block_slot // 128 equal to any one shard, and in every draw some shard gets exactly 8 from every device. `block_slot`: A permutation of the 1024 slots.
All inputs are finite; a program needn't handle non-finite values.
Results may differ from a plain program's by a relative error of at most 0.0037.
Values may be sent and summed in bfloat16 or wider, within the bound.
A program may use at most 128 MiB of HBM per device.

v0:
```python
import jax
import jax.numpy as jnp
from jax import lax
from jax.sharding import PartitionSpec as P

TABLES = 26
CAP = 8
beta_one = 0.9
beta_two = 0.999
corr_first = 1.0 - 0.9**10
corr_second = 1.0 - 0.999**10
adam_eps = 1e-06
decay_rate = 0.01
learn_rate = 0.1
ratio_eps = 1e-06


def silu_slope(pre_value):
    logistic = jax.nn.sigmoid(pre_value)
    return logistic * (1.0 + pre_value * (1.0 - logistic))


def tower_grads(dense_x, dense_cot, w_one, w_two, w_three):
    w_one_bf = w_one.astype(jnp.bfloat16)
    w_two_bf = w_two.astype(jnp.bfloat16)
    w_three_bf = w_three.astype(jnp.bfloat16)
    pre_one = lax.dot_general(
        dense_x, w_one_bf, (((0,), (0,)), ((), ())), preferred_element_type=jnp.float32
    )
    hidden_one = jax.nn.silu(pre_one).astype(jnp.bfloat16)
    pre_two = jnp.dot(hidden_one, w_two_bf, preferred_element_type=jnp.float32)
    hidden_two = jax.nn.silu(pre_two).astype(jnp.bfloat16)
    grad_three = lax.dot_general(
        hidden_two, dense_cot, (((0,), (0,)), ((), ())), preferred_element_type=jnp.float32
    )
    back_two = (
        lax.dot_general(
            dense_cot, w_three_bf, (((1,), (1,)), ((), ())), preferred_element_type=jnp.float32
        )
        * silu_slope(pre_two)
    ).astype(jnp.bfloat16)
    grad_two = lax.dot_general(
        hidden_one, back_two, (((0,), (0,)), ((), ())), preferred_element_type=jnp.float32
    )
    back_one = (
        lax.dot_general(
            back_two, w_two_bf, (((1,), (1,)), ((), ())), preferred_element_type=jnp.float32
        )
        * silu_slope(pre_one)
    ).astype(jnp.bfloat16)
    grad_one = jnp.dot(dense_x, back_one, preferred_element_type=jnp.float32)
    return (grad_one, grad_two, grad_three)


def lamb_dense(weight, first_in, second_in, gradient):
    first_out = beta_one * first_in + (1.0 - beta_one) * gradient
    second_out = beta_two * second_in + (1.0 - beta_two) * gradient * gradient
    update = (
        first_out / corr_first / (jnp.sqrt(second_out / corr_second) + adam_eps)
        + decay_rate * weight
    )
    trust_ratio = jnp.sqrt(jnp.sum(weight * weight)) / (
        jnp.sqrt(jnp.sum(update * update)) + ratio_eps
    )
    return (weight - learn_rate * trust_ratio * update, first_out, second_out)


def body(
    table,
    table_first,
    table_second,
    slot_table,
    touched,
    emb_grads,
    block_slot,
    dense_x,
    dense_cot,
    w_one,
    w_two,
    w_three,
    first_one,
    first_two,
    first_three,
    second_one,
    second_two,
    second_three,
):
    shards = lax.axis_size("shard")
    local_blocks = table.shape[0]
    block_rows = table.shape[1]
    emb_width = table.shape[2]
    row_width = block_rows * emb_width
    capacity = CAP
    dense_terms = tower_grads(dense_x, dense_cot, w_one, w_two, w_three)
    table_hot = (slot_table[:, None] == jnp.arange(TABLES, dtype=jnp.int32)[None, :]).astype(
        jnp.float32
    )
    row_weight = jnp.sum(table * table, axis=(1, 2))
    part_weight = jnp.dot(row_weight, table_hot, precision=lax.Precision.HIGHEST)
    block_ids = touched[0]
    count_touched = block_ids.shape[0]
    grad_rows = emb_grads[0].reshape(count_touched, row_width)
    slot_index = jnp.take(block_slot, block_ids)
    owner_shard = slot_index // local_blocks
    local_row = slot_index % local_blocks
    owner_hot = (owner_shard[:, None] == jnp.arange(shards, dtype=jnp.int32)[None, :]).astype(
        jnp.int32
    )
    bucket_rank = jnp.cumsum(owner_hot, axis=0) - 1
    bucket_place = jnp.sum(owner_hot * bucket_rank, axis=1)
    send_index = owner_shard * capacity + bucket_place
    picker = jnp.arange(shards * capacity, dtype=jnp.int32)[:, None] == send_index[None, :]
    send_rows = jnp.dot(
        picker.astype(jnp.bfloat16), grad_rows, preferred_element_type=jnp.float32
    ).astype(jnp.bfloat16)
    send_local = jnp.where(
        jnp.any(picker, axis=1), jnp.sum(jnp.where(picker, local_row[None, :], 0), axis=1), -1
    )
    send_rows = send_rows.reshape(shards, capacity, row_width)
    send_local = send_local.reshape(shards, capacity)
    recv_rows, recv_local = (
        lax.all_to_all(send_rows, "shard", split_axis=0, concat_axis=0, tiled=True),
        lax.all_to_all(send_local, "shard", split_axis=0, concat_axis=0, tiled=True),
    )
    piece_rows = lax.all_gather(recv_rows, "grp", axis=0, tiled=True).reshape(-1, row_width)
    piece_locals = lax.all_gather(recv_local, "grp", axis=0, tiled=True).reshape(-1)
    matches = piece_locals[:, None] == jnp.arange(local_blocks, dtype=jnp.int32)[None, :]
    summed = lax.dot_general(
        matches.astype(jnp.bfloat16),
        piece_rows,
        (((0,), (0,)), ((), ())),
        preferred_element_type=jnp.float32,
    )
    counted = jnp.sum(matches.astype(jnp.float32), axis=0)
    emb_grad = summed.reshape(local_blocks, block_rows, emb_width)
    touched_mask = (counted > 0.5)[:, None, None]
    new_first = jnp.where(
        touched_mask, beta_one * table_first + (1.0 - beta_one) * emb_grad, table_first
    )
    new_second = jnp.where(
        touched_mask, beta_two * table_second + (1.0 - beta_two) * emb_grad * emb_grad, table_second
    )
    update = jnp.where(
        touched_mask,
        new_first / corr_first / (jnp.sqrt(new_second / corr_second) + adam_eps)
        + decay_rate * table,
        0.0,
    )
    row_update = jnp.sum(update * update, axis=(1, 2))
    part_update = jnp.dot(row_update, table_hot, precision=lax.Precision.HIGHEST)
    dense_grads = lax.psum((dense_terms[0], dense_terms[1], dense_terms[2]), ("grp", "shard"))
    weight_total, update_total = lax.psum((part_weight, part_update), "shard")
    table_ratio = jnp.sqrt(weight_total) / (jnp.sqrt(update_total) + ratio_eps)
    ratio_rows = jnp.dot(table_hot, table_ratio, precision=lax.Precision.HIGHEST)
    new_table = table - learn_rate * ratio_rows[:, None, None] * update
    layer_one = lamb_dense(w_one, first_one, second_one, dense_grads[0])
    layer_two = lamb_dense(w_two, first_two, second_two, dense_grads[1])
    layer_three = lamb_dense(w_three, first_three, second_three, dense_grads[2])
    return (
        new_table,
        new_first,
        new_second,
        layer_one[0],
        layer_two[0],
        layer_three[0],
        layer_one[1],
        layer_two[1],
        layer_three[1],
        layer_one[2],
        layer_two[2],
        layer_three[2],
    )


def solution(mesh):
    return jax.shard_map(
        body,
        mesh=mesh,
        in_specs=(
            P("shard", None, None),
            P("shard", None, None),
            P("shard", None, None),
            P("shard"),
            P("grp", "shard"),
            P("grp", "shard", None, None),
            P(),
            P(None, ("grp", "shard")),
            P(("grp", "shard"), None),
            P(),
            P(),
            P(),
            P(),
            P(),
            P(),
            P(),
            P(),
            P(),
        ),
        out_specs=(
            P("shard", None, None),
            P("shard", None, None),
            P("shard", None, None),
            P(),
            P(),
            P(),
            P(),
            P(),
            P(),
            P(),
            P(),
            P(),
        ),
        check_vma=False,
    )
```

profile of v0, /device:TPU:0, one launch (start us, length us, event | category | flops | bytes accessed | tf_op | source)
XLA Modules:
  0.0 179.8 jit_solution(11988659728228566340)
XLA Ops:
  7.2 0.7 fusion.31
  7.9 1.4 gather_fusion
  9.3 0.7 and_select_fusion.1
  10.0 0.7 fusion.30
  10.7 0.1 fusion.27
  10.7 0.1 reduce_window_sum.11
  10.8 0.2 select_reduce_fusion.1
  11.0 0.1 fusion.28
  11.1 0.1 select_reduce_fusion
  11.2 0.7 select_n.94
  11.9 5.2 %all-to-all-start = ((s32[8,1,8]{2,1,0:T(1,128)}), s32[8,1,8]{2,1,0:T(1,128)S(1)}, u32[]{:S(2)}, u32[]{:S(2)}) async-start(s32[8,1,8]{2,1,0:T(1,128)} %bitcast.9), calls=%async_computation | async-start | bytes 8192 | tf_op jit(solution)/shard_map/all_to_all | solution.py:123
  17.1 6.6 %multiply_convert_fusion.1 = (bf16[4096,512]{1,0:T(8,128)(2,1)S(1)}, f32[4096,512]{1,0:T(8,128)}) fusion(bf16[13,4096]{1,0:T(8,128)(2,1)} %param.25, f32[13,512]{1,0:T(8,128)} %param.27), kind=kOutput, calls=%fused_computation.2 | convolution fusion | flops 65018368 | bytes 12716032 | tf_op jit(solution)/shard_map/dot_general | solution.py:27
  23.7 1.3 fusion.12
  25.0 2.0 %fusion.1 = f32[256,128]{1,0:T(8,128)} fusion(bf16[4096,128]{1,0:T(8,128)(2,1)S(1)} %copy-done, f32[4096,256]{1,0:T(8,128)S(1)} %fusion.12), kind=kOutput, calls=%fused_computation.8 | convolution fusion | flops 273678336 | bytes 5373952 | tf_op jit(solution)/shard_map/dot_general | solution.py:33
  26.9 1.7 fusion
  28.7 1.4 copy-done.19
  30.1 2.1 %fusion.46 = f32[512,256]{1,0:T(8,128)} fusion(bf16[4096,512]{1,0:T(8,128)(2,1)S(1)} %get-tuple-element.94, bf16[4096,256]{1,0:T(8,128)(2,1)S(1)} %fusion), kind=kOutput, calls=%fused_computation.101 | convolution fusion | flops 1073741824 | bytes 6815744 | tf_op jit(solution)/shard_map/dot_general | solution.py:42
  32.2 0.2 copy.79
  32.4 1.0 multiply_reduce_fusion.3
  33.5 1.0 fusion.3
  34.5 7.7 %fusion.4 = f32[13,512]{1,0:T(8,128)S(1)} fusion(bf16[13,4096]{1,0:T(8,128)(2,1)} %param.25, f32[4096,512]{1,0:T(8,128)} %get-tuple-element.95, bf16[4096,256]{1,0:T(8,128)(2,1)} %copy-done.19, f32[512,256]{1,0:T(8,128)S(1)} %copy-done.1), kind=kOutput, calls=%fused_computation.12 | convolution fusion | flops 1147273216 | bytes 11143168 | tf_op jit(solution)/shard_map/dot_general | solution.py:51
  42.1 41.0 %psum.37 = f32[13,512]{1,0:T(8,128)S(1)} all-reduce(f32[13,512]{1,0:T(8,128)S(1)} %fusion.4), channel_id=1, replica_groups=mesh['grp'=4,'shard'=8] {'grp','shard'}, use_global_device_ids=true, to_apply=%region_10.11 | all-reduce | flops 6656 | bytes 53248 | tf_op jit(solution)/shard_map/psum | solution.py:151
  83.2 0.6 multiply_reduce_fusion.6
  85.2 0.2 convolution_bitcast_fusion.2
  85.5 0.6 multiply_subtract_fusion.3
  86.2 1.0 copy.73
  87.2 0.2 copy.76
  87.4 3.6 %all-to-all-start.1 = ((bf16[8,8,1024]{2,1,0:T(8,128)(2,1)}), bf16[8,8,1024]{2,1,0:T(8,128)(2,1)S(1)}, u32[]{:S(2)}, u32[]{:S(2)}) async-start(bf16[8,8,1024]{2,1,0:T(8,128)(2,1)} %fusion.3), calls=%async_computation.1 | async-start | bytes 262144 | tf_op jit(solution)/shard_map/all_to_all | solution.py:122
  91.0 13.2 %all-gather = s32[32,1,8]{2,1,0:T(1,128)S(1)} all-gather(s32[8,1,8]{2,1,0:T(1,128)S(1)} %all-to-all-done), channel_id=2, replica_groups=mesh['grp'=4,'shard'=8] {'grp'}, dimensions={0}, use_global_device_ids=true | all-gather | bytes 1280 | tf_op jit(solution)/shard_map/all_gather | solution.py:126
  104.2 0.5 broadcast.168
  104.7 0.7 reduce.3
  105.4 0.1 eq.68
  105.5 0.1 convert_reduce_fusion
  105.7 16.0 %all_gather.7 = bf16[32,8,1024]{2,1,0:T(8,128)(2,1)S(1)} all-gather(bf16[8,8,1024]{2,1,0:T(8,128)(2,1)S(1)} %all-to-all-done.1), channel_id=1, replica_groups=mesh['grp'=4,'shard'=8] {'grp'}, dimensions={0}, use_global_device_ids=true | all-gather | bytes 655360 | tf_op jit(solution)/shard_map/all_gather | solution.py:125
  121.7 1.0 copy.74
  122.7 2.9 %multiply_reduce_fusion.2 = (f32[128]{0:T(128)S(1)}, f32[128,8,128]{0,2,1:T(8,128)}, f32[128,8,128]{0,2,1:T(8,128)}, f32[128,8,128]{0,2,1:T(8,128)S(1)}) fusion(f32[128,8,128]{0,2,1:T(8,128)S(1)} %copy.79, pred[128]{0:T(512)(128)(4,1)S(1)} %broadcast_compare_fusion, f32[128,8,128]{0,2,1:T(8,128)} %copy.73, f32[128,8,128]{0,2,1:T(8,128)S(1)} %copy.76, ...), kind=kOutput, calls=%fused_computation.28 | convolution fusion | flops 69500800 | bytes 3671680 | tf_op jit(solution)/shard_map/dot_general | solution.py:128
  125.6 0.2 convolution_bitcast_fusion.1
  125.8 11.8 %all-reduce.1 = (f32[26]{0:T(128)S(1)}, f32[26]{0:T(128)S(1)}) all-reduce(f32[26]{0:T(128)S(1)} %convolution_bitcast_fusion.1, f32[26]{0:T(128)S(1)} %convolution_bitcast_fusion.2), channel_id=1, replica_groups=mesh['grp'=4,'shard'=8] {'shard'}, use_global_device_ids=true, to_apply=%region_8.9 | all-reduce | flops 52 | bytes 416 | tf_op jit(solution)/shard_map/psum | solution.py:152
  137.6 0.3 fusion.5
  137.8 1.1 multiply_subtract_fusion.1
  138.9 1.0 copy.80
  139.9 2.0 %copy.81 = f32[128,8,128]{2,1,0:T(8,128)} copy(f32[128,8,128]{0,2,1:T(8,128)} %get-tuple-element.90) | data formatting | bytes 1048576
  142.0 1.0 copy.82
  143.0 21.3 %all-reduce.4.cloned.1.call-done = (f32[512,256]{1,0:T(8,128)}, f32[256,128]{1,0:T(8,128)}) async-done(((f32[512,256]{1,0:T(8,128)}, f32[256,128]{1,0:T(8,128)}), (f32[512,256]{1,0:T(8,128)}, f32[256,128]{1,0:T(8,128)})) %all-reduce.4.cloned.1.call-update) | async-done | bytes 655376 | tf_op jit(solution)/shard_map/psum | solution.py:151
  164.2 2.4 %multiply_reduce_fusion = (f32[]{:T(128)}, f32[]{:T(128)}, f32[512,256]{1,0:T(8,128)S(1)}, f32[512,256]{1,0:T(8,128)S(1)}) fusion(f32[512,256]{1,0:T(8,128)S(1)} %copy-done.1, f32[512,256]{1,0:T(8,128)} %get-tuple-element.78, f32[512,256]{1,0:T(8,128)} %param.31, f32[512,256]{1,0:T(8,128)} %param.34), kind=kLoop, calls=%fused_computation.23 | loop fusion | flops 2228222 | bytes 3145736 | tf_op jit(solution)/shard_map/reduce_sum | solution.py:63
  168.1 1.6 multiply_reduce_fusion.4
  171.1 1.1 multiply_subtract_fusion
  172.2 0.7 multiply_subtract_fusion.2
  (47 shorter events, 0.2 us)
Async XLA Ops:
  7.2 17.8 %copy-start = (bf16[4096,128]{1,0:T(8,128)(2,1)S(1)}, bf16[4096,128]{1,0:T(8,128)(2,1)}, u32[]{:S(2)}) copy-start(bf16[4096,128]{1,0:T(8,128)(2,1)} %param.26) | copy-start | bytes 3145732
  11.9 75.5 %all-to-all-start = ((s32[8,1,8]{2,1,0:T(1,128)}), s32[8,1,8]{2,1,0:T(1,128)S(1)}, u32[]{:S(2)}, u32[]{:S(2)}) async-start(s32[8,1,8]{2,1,0:T(1,128)} %bitcast.9), calls=%async_computation | async-start | bytes 8192 | tf_op jit(solution)/shard_map/all_to_all | solution.py:123
  17.1 6.6 %copy-start.1 = (f32[512,256]{1,0:T(8,128)S(1)}, f32[512,256]{1,0:T(8,128)}, u32[]{:S(2)}) copy-start(f32[512,256]{1,0:T(8,128)} %param.28) | copy-start | bytes 1572868
  17.1 147.2 %all-reduce.4.cloned.1.call-start = ((), (), s32[]{:S(2)}) async-start(), calls=%async_computation.2 | async-start | bytes 1310720 | tf_op jit(solution)/shard_map/psum | solution.py:151
  25.0 2.0 %copy-start.7 = (f32[256,128]{1,0:T(8,128)S(1)}, f32[256,128]{1,0:T(8,128)}, u32[]{:S(2)}) copy-start(f32[256,128]{1,0:T(8,128)} %param.29) | copy-start | bytes 393220
  28.7 1.4 copy-start.19
  30.1 2.1 %copy-start.2 = (f32[128,8,128]{2,1,0:T(8,128)S(1)}, f32[128,8,128]{2,1,0:T(8,128)}, u32[]{:S(2)}) copy-start(f32[128,8,128]{2,1,0:T(8,128)} %param.18) | copy-start | bytes 1572868
  30.1 3.4 %copy-start.15 = (bf16[1,32,8,128]{3,2,1,0:T(8,128)(2,1)S(1)}, bf16[1,32,8,128]{3,2,1,0:T(8,128)(2,1)}, u32[]{:S(2)}) copy-start(bf16[1,32,8,128]{3,2,1,0:T(8,128)(2,1)} %param.23) | copy-start | bytes 196612
  34.4 48.7 %copy-start.12 = (f32[13,512]{1,0:T(8,128)S(1)}, f32[13,512]{1,0:T(8,128)}, u32[]{:S(2)}) copy-start(f32[13,512]{1,0:T(8,128)} %param.27) | copy-start | bytes 79876
  34.4 48.7 %copy-start.16 = (f32[13,512]{1,0:T(8,128)S(1)}, f32[13,512]{1,0:T(8,128)}, u32[]{:S(2)}) copy-start(f32[13,512]{1,0:T(8,128)} %param.30) | copy-start | bytes 79876
  34.4 48.8 %copy-start.17 = (f32[13,512]{1,0:T(8,128)S(1)}, f32[13,512]{1,0:T(8,128)}, u32[]{:S(2)}) copy-start(f32[13,512]{1,0:T(8,128)} %param.33) | copy-start | bytes 79876
  34.4 50.8 %copy-start.18 = (s32[128]{0:T(128)S(1)}, s32[128]{0:T(128)}, u32[]{:S(2)}) copy-start(s32[128]{0:T(128)} %param.21) | copy-start | bytes 1540
  34.4 51.7 %copy-start.5 = (f32[128,8,128]{2,1,0:T(8,128)S(1)}, f32[128,8,128]{2,1,0:T(8,128)}, u32[]{:S(2)}) copy-start(f32[128,8,128]{2,1,0:T(8,128)} %param.19) | copy-start | bytes 1572868
  34.4 52.7 %copy-start.6 = (f32[128,8,128]{2,1,0:T(8,128)S(1)}, f32[128,8,128]{2,1,0:T(8,128)}, u32[]{:S(2)}) copy-start(f32[128,8,128]{2,1,0:T(8,128)} %param.20) | copy-start | bytes 1572868
  83.8 21.8 %copy-start.13 = (f32[13,512]{1,0:T(8,128)}, f32[13,512]{1,0:T(8,128)S(1)}, u32[]{:S(2)}) copy-start(f32[13,512]{1,0:T(8,128)S(1)} %get-tuple-element.86) | copy-start | bytes 79876
  83.8 21.8 %copy-start.14 = (f32[13,512]{1,0:T(8,128)}, f32[13,512]{1,0:T(8,128)S(1)}, u32[]{:S(2)}) copy-start(f32[13,512]{1,0:T(8,128)S(1)} %get-tuple-element.87) | copy-start | bytes 79876
  87.4 18.2 %all-to-all-start.1 = ((bf16[8,8,1024]{2,1,0:T(8,128)(2,1)}), bf16[8,8,1024]{2,1,0:T(8,128)(2,1)S(1)}, u32[]{:S(2)}, u32[]{:S(2)}) async-start(bf16[8,8,1024]{2,1,0:T(8,128)(2,1)} %fusion.3), calls=%async_computation.1 | async-start | bytes 262144 | tf_op jit(solution)/shard_map/all_to_all | solution.py:122
  125.6 42.5 %copy-start.10 = (f32[256,128]{1,0:T(8,128)S(1)}, f32[256,128]{1,0:T(8,128)}, u32[]{:S(2)}) copy-start(f32[256,128]{1,0:T(8,128)} %param.32) | copy-start | bytes 393220
  125.6 42.5 %copy-start.11 = (f32[256,128]{1,0:T(8,128)S(1)}, f32[256,128]{1,0:T(8,128)}, u32[]{:S(2)}) copy-start(f32[256,128]{1,0:T(8,128)} %param.35) | copy-start | bytes 393220
  166.6 6.3 %copy-start.3 = (f32[512,256]{1,0:T(8,128)}, f32[512,256]{1,0:T(8,128)S(1)}, u32[]{:S(2)}) copy-start(f32[512,256]{1,0:T(8,128)S(1)} %get-tuple-element.84) | copy-start | bytes 1572868
  166.6 6.3 %copy-start.4 = (f32[512,256]{1,0:T(8,128)}, f32[512,256]{1,0:T(8,128)S(1)}, u32[]{:S(2)}) copy-start(f32[512,256]{1,0:T(8,128)S(1)} %get-tuple-element.85) | copy-start | bytes 1572868
  169.7 3.2 %copy-start.8 = (f32[256,128]{1,0:T(8,128)}, f32[256,128]{1,0:T(8,128)S(1)}, u32[]{:S(2)}) copy-start(f32[256,128]{1,0:T(8,128)S(1)} %get-tuple-element.82) | copy-start | bytes 393220
  169.7 3.2 %copy-start.9 = (f32[256,128]{1,0:T(8,128)}, f32[256,128]{1,0:T(8,128)S(1)}, u32[]{:S(2)}) copy-start(f32[256,128]{1,0:T(8,128)S(1)} %get-tuple-element.83) | copy-start | bytes 393220
Sparse Core Ops, SparseCore 0:
  32.3 131.8 all-reduce.3
where the time goes:
time: 180 us
  blocking collectives  82 us (46%)
  matrix products  25.8 us (14%)
  waiting for transfers between devices  21.3 us (12%)
  between operations  18.6 us (10%)
  other arithmetic  12.7 us (7%)
  local copies, waits for them, and re-layouts  10.6 us (6%)
  starting transfers between devices  8.81 us (5%)
    psum x1, blocking collectives, body(): lax.psum((dense_terms[0], dense_terms[1], dense_terms[2]), ('grp', 'shard'))  41 us
    psum x1, waiting for transfers between devices, body(): lax.psum((dense_terms[0], dense_terms[1], dense_terms[2]), ('grp', 'shard'))  21.3 us
    all_gather x1, blocking collectives, body(): lax.all_gather(recv_rows, 'grp', axis=0, tiled=True).reshape(-1, row_width)  16 us
    all_gather x1, blocking collectives, body(): lax.all_gather(recv_local, 'grp', axis=0, tiled=True).reshape(-1)  13.2 us
    psum x1, blocking collectives, body(): weight_total, update_total = lax.psum((part_weight, part_update), 'shard')  11.8 us
    dot_general x1, matrix products, tower_grads(): grad_one = jnp.dot(dense_x, back_one, preferred_element_type=jnp.float32)  7.68 us
    unnamed x46, local copies, waits for them, and re-layouts  6.98 us
    dot_general x1, matrix products, tower_grads(): lax.dot_general(dense_x, w_one_bf, (((0,), (0,)), ((), ())), preferred_el...  6.56 us
  transfers between devices with their start and end apart: 3, of which 1 were waited for; matrix products, arithmetic and copies ran while one was open for 21% of the time, Pallas kernels for 0%

commit v1 on v0

--- a/solution.py
+++ b/solution.py
@@ -148,7 +148,9 @@
     )
     row_update = jnp.sum(update * update, axis=(1, 2))
     part_update = jnp.dot(row_update, table_hot, precision=lax.Precision.HIGHEST)
-    dense_grads = lax.psum((dense_terms[0], dense_terms[1], dense_terms[2]), ("grp", "shard"))
+    dense_grads = (dense_terms[0], dense_terms[1], dense_terms[2])
+    for no in ("shard", "grp"):
+        dense_grads = lax.psum(dense_grads, no)
     weight_total, update_total = lax.psum((part_weight, part_update), "shard")
     table_ratio = jnp.sqrt(weight_total) / (jnp.sqrt(update_total) + ratio_eps)
     ratio_rows = jnp.dot(table_hot, table_ratio, precision=lax.Precision.HIGHEST)

time: 180 us -> 183 us (1.017)
  blocking collectives: 82 us -> 71 us
  waiting for transfers between devices: 21.3 us -> 31.2 us
  other arithmetic: 12.7 us -> 14.9 us
    psum x1, blocking collectives: 41 us -> 18.2 us  [body(): dense_grads = lax.psum(dense_grads, no)]
    psum x1, blocking collectives: 11.8 us -> 23.9 us  [body(): weight_total, update_total = lax.psum((part_weight, part_update), 'shard')]
    psum x1 -> x2, waiting for transfers between devices: 21.3 us -> 31.2 us  [body(): dense_grads = lax.psum(dense_grads, no)]
    unnamed x46 -> x38, local copies, waits for them, and re-layouts: 6.98 us -> 7.01 us
  transfers between devices with their start and end apart: 3 -> 4, of which waited for: 1 -> 1; matrix products, arithmetic and copies ran while one was open for 21% -> 22% of each run, Pallas kernels for 0% -> 0%
where the time goes in v1:
time: 183 us; the launch traced here: 182 us
  blocking collectives  71 us (39%)
  waiting for transfers between devices  31.2 us (17%)
  matrix products  26.4 us (14%)
  between operations  18.5 us (10%)
  other arithmetic  14.9 us (8%)
  local copies, waits for them, and re-layouts  10.7 us (6%)
  starting transfers between devices  9.45 us (5%)
    psum x2, waiting for transfers between devices, body(): dense_grads = lax.psum(dense_grads, no)  31.2 us
    psum x1, blocking collectives, body(): weight_total, update_total = lax.psum((part_weight, part_update), 'shard')  23.9 us
    psum x1, blocking collectives, body(): dense_grads = lax.psum(dense_grads, no)  18.2 us
    all_gather x1, blocking collectives, body(): lax.all_gather(recv_rows, 'grp', axis=0, tiled=True).reshape(-1, row_width)  15.5 us
    all_gather x1, blocking collectives, body(): lax.all_gather(recv_local, 'grp', axis=0, tiled=True).reshape(-1)  13.4 us
    dot_general x1, matrix products, tower_grads(): grad_one = jnp.dot(dense_x, back_one, preferred_element_type=jnp.float32)  8.35 us
    unnamed x38, local copies, waits for them, and re-layouts  7.01 us
    dot_general x1, matrix products, tower_grads(): lax.dot_general(dense_x, w_one_bf, (((0,), (0,)), ((), ())), preferred_el...  6.56 us
  transfers between devices with their start and end apart: 4, of which 1 were waited for; matrix products, arithmetic and copies ran while one was open for 22% of the time, Pallas kernels for 0%

profile of v1, /device:TPU:0, one launch (start us, length us, event | category | flops | bytes accessed | tf_op | source)
XLA Modules:
  0.0 182.1 jit_solution(14921380239094980243)
XLA Ops:
  7.2 0.7 fusion.31
  7.9 1.4 gather_fusion
  9.3 0.7 and_select_fusion.1
  10.0 0.7 fusion.30
  10.7 0.1 fusion.27
  10.7 0.1 reduce_window_sum.11
  10.8 0.2 select_reduce_fusion.1
  11.0 0.1 fusion.28
  11.1 0.1 select_reduce_fusion
  11.2 0.7 select_n.94
  11.9 5.2 %all-to-all-start = ((s32[8,1,8]{2,1,0:T(1,128)}), s32[8,1,8]{2,1,0:T(1,128)S(1)}, u32[]{:S(2)}, u32[]{:S(2)}) async-start(s32[8,1,8]{2,1,0:T(1,128)} %bitcast.9), calls=%async_computation | async-start | bytes 8192 | tf_op jit(solution)/shard_map/all_to_all | solution.py:123
  17.1 6.6 %multiply_convert_fusion.1 = (bf16[4096,512]{1,0:T(8,128)(2,1)S(1)}, f32[4096,512]{1,0:T(8,128)}) fusion(bf16[13,4096]{1,0:T(8,128)(2,1)} %param.25, f32[13,512]{1,0:T(8,128)} %param.27), kind=kOutput, calls=%fused_computation.2 | convolution fusion | flops 65018368 | bytes 12716032 | tf_op jit(solution)/shard_map/dot_general | solution.py:27
  23.7 1.3 fusion.12
  25.0 2.0 %fusion.1 = f32[256,128]{1,0:T(8,128)} fusion(bf16[4096,128]{1,0:T(8,128)(2,1)S(1)} %copy-done, f32[4096,256]{1,0:T(8,128)S(1)} %fusion.12), kind=kOutput, calls=%fused_computation.8 | convolution fusion | flops 273678336 | bytes 5373952 | tf_op jit(solution)/shard_map/dot_general | solution.py:33
  26.9 1.7 fusion
  28.7 1.4 copy-done.15
  30.1 2.1 %fusion.46 = f32[512,256]{1,0:T(8,128)} fusion(bf16[4096,512]{1,0:T(8,128)(2,1)S(1)} %get-tuple-element.97, bf16[4096,256]{1,0:T(8,128)(2,1)S(1)} %fusion), kind=kOutput, calls=%fused_computation.101 | convolution fusion | flops 1073741824 | bytes 6815744 | tf_op jit(solution)/shard_map/dot_general | solution.py:42
  32.2 0.2 copy.79
  32.4 1.0 multiply_reduce_fusion.3
  33.5 1.0 fusion.3
  34.4 8.4 %fusion.4 = f32[13,512]{1,0:T(8,128)} fusion(bf16[13,4096]{1,0:T(8,128)(2,1)S(1)} %copy-done.13, f32[4096,512]{1,0:T(8,128)} %get-tuple-element.98, bf16[4096,256]{1,0:T(8,128)(2,1)} %copy-done.15, f32[512,256]{1,0:T(8,128)S(1)} %copy-done.1), kind=kOutput, calls=%fused_computation.12 | convolution fusion | flops 1147273216 | bytes 11143168 | tf_op jit(solution)/shard_map/dot_general | solution.py:51
  42.8 0.2 convolution_bitcast_fusion.2
  43.0 1.1 copy.73
  44.0 0.2 copy.76
  44.3 4.2 %all-to-all-start.1 = ((bf16[8,8,1024]{2,1,0:T(8,128)(2,1)}), bf16[8,8,1024]{2,1,0:T(8,128)(2,1)S(1)}, u32[]{:S(2)}, u32[]{:S(2)}) async-start(bf16[8,8,1024]{2,1,0:T(8,128)(2,1)} %fusion.3), calls=%async_computation.1 | async-start | bytes 262144 | tf_op jit(solution)/shard_map/all_to_all | solution.py:122
  48.5 13.4 %all-gather = s32[32,1,8]{2,1,0:T(1,128)S(1)} all-gather(s32[8,1,8]{2,1,0:T(1,128)S(1)} %all-to-all-done), channel_id=2, replica_groups=mesh['grp'=4,'shard'=8] {'grp'}, dimensions={0}, use_global_device_ids=true | all-gather | bytes 1280 | tf_op jit(solution)/shard_map/all_gather | solution.py:126
  61.9 0.5 broadcast.168
  62.4 0.7 reduce.3
  63.1 0.1 eq.68
  63.2 0.1 convert_reduce_fusion
  63.4 15.5 %all_gather.7 = bf16[32,8,1024]{2,1,0:T(8,128)(2,1)S(1)} all-gather(bf16[8,8,1024]{2,1,0:T(8,128)(2,1)S(1)} %all-to-all-done.1), channel_id=1, replica_groups=mesh['grp'=4,'shard'=8] {'grp'}, dimensions={0}, use_global_device_ids=true | all-gather | bytes 655360 | tf_op jit(solution)/shard_map/all_gather | solution.py:125
  78.8 1.0 copy.74
  79.8 2.9 %multiply_reduce_fusion.2 = (f32[128]{0:T(128)S(1)}, f32[128,8,128]{0,2,1:T(8,128)}, f32[128,8,128]{0,2,1:T(8,128)}, f32[128,8,128]{0,2,1:T(8,128)S(1)}) fusion(f32[128,8,128]{0,2,1:T(8,128)S(1)} %copy.79, pred[128]{0:T(512)(128)(4,1)S(1)} %broadcast_compare_fusion, f32[128,8,128]{0,2,1:T(8,128)} %copy.73, f32[128,8,128]{0,2,1:T(8,128)S(1)} %copy.76, ...), kind=kOutput, calls=%fused_computation.28 | convolution fusion | flops 69500800 | bytes 3671680 | tf_op jit(solution)/shard_map/dot_general | solution.py:128
  82.8 0.2 convolution_bitcast_fusion.1
  82.9 23.9 %all-reduce = (f32[26]{0:T(128)S(1)}, f32[26]{0:T(128)S(1)}, f32[13,512]{1,0:T(8,128)S(1)}) all-reduce(f32[26]{0:T(128)S(1)} %convolution_bitcast_fusion.1, f32[26]{0:T(128)S(1)} %convolution_bitcast_fusion.2, f32[13,512]{1,0:T(8,128)} %fusion.4), channel_id=1, replica_groups=mesh['grp'=4,'shard'=8] {'shard'}, use_global_device_ids=true, to_apply=%region_8.9 | all-reduce | flops 6708 | bytes 53664 | tf_op jit(solution)/shard_map/psum | solution.py:154
  106.8 18.2 %psum.59 = f32[13,512]{1,0:T(8,128)S(1)} all-reduce(f32[13,512]{1,0:T(8,128)S(1)} %get-tuple-element.80), channel_id=1, replica_groups=mesh['grp'=4,'shard'=8] {'grp'}, use_global_device_ids=true, to_apply=%region_11.12 | all-reduce | flops 6656 | bytes 53248 | tf_op jit(solution)/shard_map/psum | solution.py:153
  125.0 2.0 %multiply_reduce_fusion.6 = (f32[]{:T(128)}, f32[]{:T(128)}, f32[13,512]{1,0:T(8,128)}, f32[13,512]{1,0:T(8,128)}) fusion(f32[13,512]{1,0:T(8,128)} %param.27, f32[13,512]{1,0:T(8,128)S(1)} %psum.59, f32[13,512]{1,0:T(8,128)} %param.30, f32[13,512]{1,0:T(8,128)} %param.33), kind=kLoop, calls=%fused_computation.54 | loop fusion | flops 113150 | bytes 159752 | tf_op jit(solution)/shard_map/reduce_sum | solution.py:63
  128.5 0.2 fusion.5
  128.7 1.2 multiply_subtract_fusion.1
  129.9 1.0 copy.80
  130.8 2.1 %copy.81 = f32[128,8,128]{2,1,0:T(8,128)} copy(f32[128,8,128]{0,2,1:T(8,128)} %get-tuple-element.93) | data formatting | bytes 1048576
  132.9 1.0 copy.82
  134.0 1.4 multiply_subtract_fusion.3
  135.4 31.2 %all-reduce.8.cloned.1.call-done = (f32[512,256]{1,0:T(8,128)}, f32[256,128]{1,0:T(8,128)}) async-done(((f32[512,256]{1,0:T(8,128)}, f32[256,128]{1,0:T(8,128)}), (f32[512,256]{1,0:T(8,128)}, f32[256,128]{1,0:T(8,128)})) %all-reduce.8.cloned.1.call-update) | async-done | bytes 655376 | tf_op jit(solution)/shard_map/psum | solution.py:153
  166.6 1.6 multiply_reduce_fusion.4
  169.6 2.4 %multiply_reduce_fusion = (f32[]{:T(128)}, f32[]{:T(128)}, f32[512,256]{1,0:T(8,128)S(1)}, f32[512,256]{1,0:T(8,128)S(1)}) fusion(f32[512,256]{1,0:T(8,128)S(1)} %copy-done.1, f32[512,256]{1,0:T(8,128)} %get-tuple-element.83, f32[512,256]{1,0:T(8,128)} %param.31, f32[512,256]{1,0:T(8,128)} %param.34), kind=kLoop, calls=%fused_computation.23 | loop fusion | flops 2228222 | bytes 3145736 | tf_op jit(solution)/shard_map/reduce_sum | solution.py:63
  173.5 0.7 multiply_subtract_fusion.2
  174.2 1.1 multiply_subtract_fusion
  (42 shorter events, 0.2 us)
Async XLA Ops:
  7.2 17.8 %copy-start = (bf16[4096,128]{1,0:T(8,128)(2,1)S(1)}, bf16[4096,128]{1,0:T(8,128)(2,1)}, u32[]{:S(2)}) copy-start(bf16[4096,128]{1,0:T(8,128)(2,1)} %param.26) | copy-start | bytes 3145732
  11.9 32.4 %all-to-all-start = ((s32[8,1,8]{2,1,0:T(1,128)}), s32[8,1,8]{2,1,0:T(1,128)S(1)}, u32[]{:S(2)}, u32[]{:S(2)}) async-start(s32[8,1,8]{2,1,0:T(1,128)} %bitcast.9), calls=%async_computation | async-start | bytes 8192 | tf_op jit(solution)/shard_map/all_to_all | solution.py:123
  17.1 6.6 %copy-start.1 = (f32[512,256]{1,0:T(8,128)S(1)}, f32[512,256]{1,0:T(8,128)}, u32[]{:S(2)}) copy-start(f32[512,256]{1,0:T(8,128)} %param.28) | copy-start | bytes 1572868
  17.1 111.4 %all-reduce.6.cloned.1.call-start = ((), (), s32[]{:S(2)}) async-start(), calls=%async_computation.2 | async-start | bytes 1310720 | tf_op jit(solution)/shard_map/psum | solution.py:153
  25.0 2.0 %copy-start.7 = (f32[256,128]{1,0:T(8,128)S(1)}, f32[256,128]{1,0:T(8,128)}, u32[]{:S(2)}) copy-start(f32[256,128]{1,0:T(8,128)} %param.29) | copy-start | bytes 393220
  28.7 1.4 copy-start.15
  30.1 2.1 %copy-start.2 = (f32[128,8,128]{2,1,0:T(8,128)S(1)}, f32[128,8,128]{2,1,0:T(8,128)}, u32[]{:S(2)}) copy-start(f32[128,8,128]{2,1,0:T(8,128)} %param.18) | copy-start | bytes 1572868
  30.1 3.4 %copy-start.12 = (bf16[1,32,8,128]{3,2,1,0:T(8,128)(2,1)S(1)}, bf16[1,32,8,128]{3,2,1,0:T(8,128)(2,1)}, u32[]{:S(2)}) copy-start(bf16[1,32,8,128]{3,2,1,0:T(8,128)(2,1)} %param.23) | copy-start | bytes 196612
  30.1 4.3 %copy-start.13 = (bf16[13,4096]{1,0:T(8,128)(2,1)S(1)}, bf16[13,4096]{1,0:T(8,128)(2,1)}, u32[]{:S(2)}) copy-start(bf16[13,4096]{1,0:T(8,128)(2,1)} %param.25) | copy-start | bytes 319492
  34.4 8.4 %copy-start.14 = (s32[128]{0:T(128)S(1)}, s32[128]{0:T(128)}, u32[]{:S(2)}) copy-start(s32[128]{0:T(128)} %param.21) | copy-start | bytes 1540
  34.4 8.6 %copy-start.5 = (f32[128,8,128]{2,1,0:T(8,128)S(1)}, f32[128,8,128]{2,1,0:T(8,128)}, u32[]{:S(2)}) copy-start(f32[128,8,128]{2,1,0:T(8,128)} %param.19) | copy-start | bytes 1572868
  34.4 9.6 %copy-start.6 = (f32[128,8,128]{2,1,0:T(8,128)S(1)}, f32[128,8,128]{2,1,0:T(8,128)}, u32[]{:S(2)}) copy-start(f32[128,8,128]{2,1,0:T(8,128)} %param.20) | copy-start | bytes 1572868
  44.3 19.1 %all-to-all-start.1 = ((bf16[8,8,1024]{2,1,0:T(8,128)(2,1)}), bf16[8,8,1024]{2,1,0:T(8,128)(2,1)S(1)}, u32[]{:S(2)}, u32[]{:S(2)}) async-start(bf16[8,8,1024]{2,1,0:T(8,128)(2,1)} %fusion.3), calls=%async_computation.1 | async-start | bytes 262144 | tf_op jit(solution)/shard_map/all_to_all | solution.py:122
  48.4 118.1 %all-reduce.8.cloned.1.call-start = ((), (), s32[]{:S(2)}) async-start(), calls=%async_computation.3 | async-start | bytes 1310720 | tf_op jit(solution)/shard_map/psum | solution.py:153
  79.8 86.7 %copy-start.10 = (f32[256,128]{1,0:T(8,128)S(1)}, f32[256,128]{1,0:T(8,128)}, u32[]{:S(2)}) copy-start(f32[256,128]{1,0:T(8,128)} %param.32) | copy-start | bytes 393220
  82.7 83.8 %copy-start.11 = (f32[256,128]{1,0:T(8,128)S(1)}, f32[256,128]{1,0:T(8,128)}, u32[]{:S(2)}) copy-start(f32[256,128]{1,0:T(8,128)} %param.35) | copy-start | bytes 393220
  168.2 7.1 %copy-start.8 = (f32[256,128]{1,0:T(8,128)}, f32[256,128]{1,0:T(8,128)S(1)}, u32[]{:S(2)}) copy-start(f32[256,128]{1,0:T(8,128)S(1)} %get-tuple-element.85) | copy-start | bytes 393220
  168.2 7.1 %copy-start.9 = (f32[256,128]{1,0:T(8,128)}, f32[256,128]{1,0:T(8,128)S(1)}, u32[]{:S(2)}) copy-start(f32[256,128]{1,0:T(8,128)S(1)} %get-tuple-element.86) | copy-start | bytes 393220
  172.0 3.2 %copy-start.3 = (f32[512,256]{1,0:T(8,128)}, f32[512,256]{1,0:T(8,128)S(1)}, u32[]{:S(2)}) copy-start(f32[512,256]{1,0:T(8,128)S(1)} %get-tuple-element.87) | copy-start | bytes 1572868
  172.0 3.2 %copy-start.4 = (f32[512,256]{1,0:T(8,128)}, f32[512,256]{1,0:T(8,128)S(1)}, u32[]{:S(2)}) copy-start(f32[512,256]{1,0:T(8,128)S(1)} %get-tuple-element.88) | copy-start | bytes 1572868
Sparse Core Ops, SparseCore 0:
  32.3 56.9 all-reduce.5
  128.6 37.9 all-reduce.7
